TPU v7x, 256 devices: a whole 4x4x8 slice. The times are simulated.
256 devices in a mesh: dp: 8 (over z), context: 32 (over y, x, core).
Axes of the slice: x: 4, y: 4, z: 8, core: 2. Of those that a mesh axis runs over, the one named last changes fastest.
Arguments:
- query_in: bfloat16 [8, 16384, 1024], P('dp', 'context'), may hold values from -6 to 6
- key_in: bfloat16 [8, 16384, 1024], P('dp', 'context'), may hold values from -6 to 6
- value_in: bfloat16 [8, 16384, 1024], P('dp', 'context'), may hold values from -6 to 6
- out_grad: bfloat16 [8, 16384, 2048], P('dp', 'context'), may hold values from -6 to 6
- out_weight: bfloat16 [1024, 2048], P('context'), may hold values from -0.1875 to 0.1875
Outputs:
- output: bfloat16 [8, 16384, 2048], P('dp', 'context')
- query_grad: bfloat16 [8, 16384, 1024], P('dp', 'context')
- key_grad: bfloat16 [8, 16384, 1024], P('dp', 'context')
- value_grad: bfloat16 [8, 16384, 1024], P('dp', 'context')
- weight_grad: float32 [1024, 2048], P('context')
All inputs are finite; a program needn't handle non-finite values.
Results may differ from a plain program's by a relative error of at most 0.025.
Values may be sent and summed in bfloat16 or wider, within the bound.
No kernel may reach another device: no remote copies, remote signals or barrier semaphores. Data moves between devices by JAX's collectives and lax.ppermute only.
A program may use at most 192 MiB of HBM per device.

v0:
```python
import math
import jax
import jax.numpy as jnp
from jax import lax
from jax.sharding import PartitionSpec as P

HEADS = 8
HEAD_DIM = 128


def prefix(value, axis, join, neutral, backward):
    count, mine = (lax.axis_size(axis), lax.axis_index(axis))
    pieces = lax.all_gather(value, axis)
    if backward:
        pieces = pieces[::-1]
        mine = count - 1 - mine
    so_far = jnp.full_like(value, 0) + jnp.asarray(neutral, value.dtype)

    def turn(position, so_far):
        longer = join(so_far, pieces[position])
        return jnp.where(position < mine, longer, so_far)

    return lax.fori_loop(0, count - 1, turn, so_far)


def add_state(earlier, later):
    return earlier + later


def on_device(query_in, key_in, value_in, out_grad, out_weight):
    tok_rows = query_in.shape[1]
    head_width = query_in.shape[2]
    contexts = lax.axis_size("context")
    groups = lax.axis_size("dp")
    att_scale = 1.0 / math.sqrt(HEAD_DIM * tok_rows * contexts)
    grad_scale = 1.0 / math.sqrt(tok_rows * contexts * groups)
    split_heads = (tok_rows, HEADS, HEAD_DIM)
    queries = query_in[0].reshape(split_heads)
    keys_here = key_in[0].reshape(split_heads)
    values_here = value_in[0].reshape(split_heads)
    grad_flat = out_grad[0]
    full_weight = lax.all_gather(out_weight, "context", axis=0, tiled=True)
    head_grad = lax.dot_general(
        grad_flat, full_weight, (((1,), (1,)), ((), ())), preferred_element_type=jnp.float32
    ).astype(jnp.bfloat16)
    grad_heads = head_grad.reshape(split_heads)
    kv_block = jnp.einsum(
        "shd,she->hde", keys_here, values_here, preferred_element_type=jnp.float32
    )
    qg_block = jnp.einsum("thd,the->hde", queries, grad_heads, preferred_element_type=jnp.float32)
    blank_state = jnp.zeros_like(kv_block)
    kv_prior = prefix(kv_block, "context", add_state, blank_state, False)
    qg_later = prefix(qg_block, "context", add_state, blank_state, True)
    kv_before = kv_prior.astype(jnp.bfloat16)
    qg_after = qg_later.astype(jnp.bfloat16)
    positions = lax.broadcasted_iota(jnp.int32, (tok_rows, tok_rows), 0)
    sources = lax.broadcasted_iota(jnp.int32, (tok_rows, tok_rows), 1)
    causal = (positions >= sources)[None]
    scores = (
        jnp.einsum("thd,shd->hts", queries, keys_here, preferred_element_type=jnp.float32)
        * att_scale
    )
    scores = jnp.where(causal, scores, 0.0).astype(jnp.bfloat16)
    attended = jnp.einsum(
        "hts,shd->thd", scores, values_here, preferred_element_type=jnp.float32
    ) + att_scale * jnp.einsum(
        "thd,hde->the", queries, kv_before, preferred_element_type=jnp.float32
    )
    attended = attended.astype(jnp.bfloat16).reshape(tok_rows, head_width)
    output = jnp.dot(attended, full_weight, preferred_element_type=jnp.float32).astype(jnp.bfloat16)
    back_scores = (
        jnp.einsum("the,she->hts", grad_heads, values_here, preferred_element_type=jnp.float32)
        * att_scale
    )
    back_scores = jnp.where(causal, back_scores, 0.0).astype(jnp.bfloat16)
    query_grad = jnp.einsum(
        "hts,shd->thd", back_scores, keys_here, preferred_element_type=jnp.float32
    ) + att_scale * jnp.einsum(
        "the,hde->thd", grad_heads, kv_before, preferred_element_type=jnp.float32
    )
    key_grad = jnp.einsum(
        "hts,thd->shd", back_scores, queries, preferred_element_type=jnp.float32
    ) + att_scale * jnp.einsum(
        "she,hde->shd", values_here, qg_after, preferred_element_type=jnp.float32
    )
    value_grad = jnp.einsum(
        "hts,the->she", scores, grad_heads, preferred_element_type=jnp.float32
    ) + att_scale * jnp.einsum(
        "shd,hde->she", keys_here, qg_after, preferred_element_type=jnp.float32
    )
    query_grad = query_grad.astype(jnp.bfloat16).reshape(tok_rows, head_width)
    key_grad = key_grad.astype(jnp.bfloat16).reshape(tok_rows, head_width)
    value_grad = value_grad.astype(jnp.bfloat16).reshape(tok_rows, head_width)
    group_part = lax.psum_scatter(
        (
            lax.dot_general(
                attended, grad_flat, (((0,), (0,)), ((), ())), preferred_element_type=jnp.float32
            )
            * grad_scale
        ).astype(jnp.bfloat16),
        "context",
        scatter_dimension=0,
        tiled=True,
    )
    weight_grad = lax.psum(group_part, "dp").astype(jnp.float32)
    return (output[None], query_grad[None], key_grad[None], value_grad[None], weight_grad)


def solution(mesh):
    placed = (
        P("dp", "context", None),
        P("dp", "context", None),
        P("dp", "context", None),
        P("dp", "context", None),
        P("context", None),
    )
    return jax.shard_map(
        on_device,
        mesh=mesh,
        in_specs=placed,
        out_specs=(
            P("dp", "context", None),
            P("dp", "context", None),
            P("dp", "context", None),
            P("dp", "context", None),
            P("context", None),
        ),
        check_vma=False,
    )
```

profile of v0, /device:TPU:1, one launch (start us, length us, event | category | flops | bytes accessed | tf_op | source)
XLA Modules:
  0.0 466.4 jit_solution(10558739906381796081)
XLA Ops:
  7.2 1.6 copy.59
  8.9 2.9 copy.58
  11.7 2.4 copy.35
  14.1 2.5 fusion.16
  17.6 2.5 copy.57
  20.0 5.0 %select_convert_fusion.1 = bf16[8,512,512]{2,1,0:T(8,128)(2,1)} fusion(pred[512,512]{1,0:T(8,128)(4,1)S(1)} %iota_compare_fusion, bf16[512,8,128]{2,1,0:T(8,128)(2,1)} %bitcast.83, bf16[512,8,128]{2,1,0:T(8,128)(2,1)} %bitcast.78), kind=kOutput, calls=%fused_computation.4 | convolution fusion | flops 543162368 | bytes 6553600 | tf_op jit(solution)/shard_map/thd,shd->hts/dot_general | solution.py:60
  25.0 73.5 %all-gather.8.cloned.1.call-done = f32[256,128,128]{2,1,0:T(8,128)} async-done(((f32[8,128,128]{2,1,0:T(8,128)}), f32[256,128,128]{2,1,0:T(8,128)}) %all-gather.8.cloned.1.call-update) | async-done | bytes 16777232 | tf_op jit(solution)/shard_map/all_gather | solution.py:13
  98.5 38.9 %while.28 = (s32[]{:T(128)}, f32[8,128,128]{2,1,0:T(8,128)S(1)}, s32[]{:T(128)}, f32[32,8,128,128]{3,2,1,0:T(8,128)}, s32[]{:T(128)}, /*index=5*/s32[]{:T(128)}) while((s32[]{:T(128)}, f32[8,128,128]{2,1,0:T(8,128)S(1)}, s32[]{:T(128)}, f32[32,8,128,128]{3,2,1,0:T(8,128)}, s32[]{:T(128)}, /*index=5*/s32[]{:T(128)}) %tuple.81), condition=%wide.region_1.2_spmd.clone, body=%wide.region_0.1_spmd.clone.sunk | while | flops 393220 | bytes 1572957 | solution.py:23
  99.8 1.2 add_select_fusion.4
  101.0 1.2 add_select_fusion.4
  102.3 1.2 add_select_fusion.4
  103.5 1.2 add_select_fusion.4
  104.8 1.2 add_select_fusion.4
  106.0 1.2 add_select_fusion.4
  107.3 1.2 add_select_fusion.4
  108.5 1.2 add_select_fusion.4
  109.8 1.2 add_select_fusion.4
  111.0 1.2 add_select_fusion.4
  112.3 1.2 add_select_fusion.4
  113.5 1.2 add_select_fusion.4
  114.8 1.2 add_select_fusion.4
  116.0 1.2 add_select_fusion.4
  117.3 1.2 add_select_fusion.4
  118.6 1.2 add_select_fusion.4
  119.8 1.2 add_select_fusion.4
  121.1 1.2 add_select_fusion.4
  122.3 1.2 add_select_fusion.4
  123.6 1.2 add_select_fusion.4
  124.8 1.2 add_select_fusion.4
  126.1 1.2 add_select_fusion.4
  127.3 1.2 add_select_fusion.4
  128.6 1.2 add_select_fusion.4
  129.8 1.2 add_select_fusion.4
  131.1 1.2 add_select_fusion.4
  132.3 1.2 add_select_fusion.4
  133.6 1.2 add_select_fusion.4
  134.9 1.3 add_select_fusion.4
  136.2 1.2 add_select_fusion.4
  137.5 1.8 fusion.21
  139.3 3.8 fusion.6
  144.2 4.3 multiply_convert_fusion
  148.6 3.2 all-gather.6.cloned.1.call-done
  151.7 5.5 %fusion.7 = bf16[512,1024]{1,0:T(8,128)(2,1)} fusion(bf16[1024,2048]{1,0:T(8,128)(2,1)} %all-gather.6.cloned.1.call-done, bf16[1,512,2048]{2,1,0:T(8,128)(2,1)S(1)} %copy-done), kind=kOutput, calls=%fused_computation.17 | convolution fusion | flops 2148007936 | bytes 7340032 | tf_op jit(solution)/shard_map/dot_general | solution.py:43
  157.3 1.6 copy.56
  158.9 83.8 %reduce-scatter.2.cloned.1.call-done = bf16[32,2048]{1,0:T(8,128)(2,1)} async-done(((bf16[1024,2048]{1,0:T(8,128)(2,1)}), bf16[32,2048]{1,0:T(8,128)(2,1)}) %reduce-scatter.2.cloned.1.call-update) | async-done | bytes 131088 | tf_op jit(solution)/shard_map/reduce_scatter | solution.py:94
  242.9 1.7 convolution_bitcast_fusion
  245.7 1.6 select_convert_fusion
  247.8 2.0 fusion.28
  250.5 1.5 fusion.2
  252.0 1.3 copy.51
  253.4 6.2 %fusion = bf16[1,512,2048]{2,1,0:T(8,128)(2,1)} fusion(bf16[512,1024]{0,1:T(8,128)(2,1)} %bitcast.92, bf16[1024,2048]{1,0:T(8,128)(2,1)} %all-gather.6.cloned.1.call-done), kind=kOutput, calls=%fused_computation.6 | convolution fusion | flops 2148532224 | bytes 7340032 | tf_op jit(solution)/shard_map/dot_general | solution.py:70
  259.6 53.3 %all-reduce.2.cloned.1.call-done = bf16[32,2048]{1,0:T(8,128)(2,1)} async-done(((bf16[32,2048]{1,0:T(8,128)(2,1)}), bf16[32,2048]{1,0:T(8,128)(2,1)}) %all-reduce.2.cloned.1.call-update) | async-done | bytes 131088 | tf_op jit(solution)/shard_map/psum | solution.py:105
  312.9 1.6 convert_element_type.51
  314.5 82.2 %all-gather.10.cloned.1.call-done = f32[256,128,128]{2,1,0:T(8,128)} async-done(((f32[8,128,128]{2,1,0:T(8,128)}), f32[256,128,128]{2,1,0:T(8,128)}) %all-gather.10.cloned.1.call-update) | async-done | bytes 16777232 | tf_op jit(solution)/shard_map/all_gather | solution.py:13
  396.7 11.6 %rev.3 = f32[32,8,128,128]{3,2,1,0:T(8,128)} reverse(f32[32,8,128,128]{3,2,1,0:T(8,128)} %bitcast.73), dimensions={0} | reverse | bytes 33554432 | tf_op jit(solution)/shard_map/rev | solution.py:15
  408.4 38.8 %while.29 = (s32[]{:T(128)}, f32[8,128,128]{2,1,0:T(8,128)S(1)}, s32[]{:T(128)}, f32[32,8,128,128]{3,2,1,0:T(8,128)}, s32[]{:T(128)}, /*index=5*/s32[]{:T(128)}) while((s32[]{:T(128)}, f32[8,128,128]{2,1,0:T(8,128)S(1)}, s32[]{:T(128)}, f32[32,8,128,128]{3,2,1,0:T(8,128)}, s32[]{:T(128)}, /*index=5*/s32[]{:T(128)}) %tuple.68), condition=%wide.region_3.4_spmd.clone, body=%wide.region_2.3_spmd.clone.sunk | while | flops 393220 | bytes 1572957 | solution.py:23
  408.4 1.3 add_select_fusion.5
  416.0 1.2 add_select_fusion.5
  426.0 1.2 add_select_fusion.5
  439.7 1.2 add_select_fusion.5
  447.7 4.1 fusion.1
  451.8 2.4 copy.52
  454.2 3.5 add_convert_fusion
  457.6 2.3 copy.53
  (64 shorter events, 39.4 us)
Async XLA Ops:
  7.2 137.0 %copy-start = (bf16[1,512,2048]{2,1,0:T(8,128)(2,1)S(1)}, bf16[1,512,2048]{2,1,0:T(8,128)(2,1)}, u32[]{:S(2)}) copy-start(bf16[1,512,2048]{2,1,0:T(8,128)(2,1)} %param.12) | copy-start | bytes 6291460
  7.2 91.3 %all-gather.8.cloned.1.call-start = ((), (), s32[]{:S(2)}) async-start(), calls=%async_computation.4 | async-start | bytes 17301504 | tf_op jit(solution)/shard_map/all_gather | solution.py:13
  8.9 8.6 %copy-start.4 = (bf16[64,8,8,128]{3,2,1,0:T(8,128)(2,1)}, bf16[64,8,8,128]{3,2,1,0:T(8,128)(2,1)S(1)}, u32[]{:S(2)}) copy-start(bf16[64,8,8,128]{3,2,1,0:T(8,128)(2,1)S(1)} %copy.59) | copy-start | bytes 3145732
  16.6 135.1 %all-gather.6.cloned.1.call-start = ((), (), s32[]{:S(2)}) async-start(), calls=%async_computation.1 | async-start | bytes 4325376 | tf_op jit(solution)/shard_map/all_gather | solution.py:42
  17.4 225.3 %reduce-scatter.2.cloned.1.call-start = ((), (), s32[]{:S(2)}) async-start(), calls=%async_computation.2 | async-start | bytes 4325376 | tf_op jit(solution)/shard_map/reduce_scatter | solution.py:94
  137.5 1.8 copy-start.5
  143.1 1.1 copy-start.9
  148.5 164.4 %all-reduce.2.cloned.1.call-start = ((), (), s32[]{:S(2)}) async-start(), calls=%async_computation.3 | async-start | bytes 262144 | tf_op jit(solution)/shard_map/psum | solution.py:105
  157.3 88.4 %copy-start.6 = (bf16[64,8,8,128]{3,2,1,0:T(8,128)(2,1)S(1)}, bf16[64,8,8,128]{3,2,1,0:T(8,128)(2,1)}, u32[]{:S(2)}) copy-start(bf16[64,8,8,128]{3,2,1,0:T(8,128)(2,1)} %copy-done.4) | copy-start | bytes 3145732
  242.7 154.0 %all-gather.10.cloned.1.call-start = ((), (), s32[]{:S(2)}) async-start(), calls=%async_computation.5 | async-start | bytes 17301504 | tf_op jit(solution)/shard_map/all_gather | solution.py:13
  245.6 2.2 copy-start.2
  247.8 2.7 copy-start.3
  247.8 2.7 copy-start.8
  408.4 39.3 %copy-start.7 = (bf16[64,8,8,128]{3,2,1,0:T(8,128)(2,1)S(1)}, bf16[64,8,8,128]{3,2,1,0:T(8,128)(2,1)}, u32[]{:S(2)}) copy-start(bf16[64,8,8,128]{3,2,1,0:T(8,128)(2,1)} %copy.57) | copy-start | bytes 3145732
  451.8 8.1 %copy-start.1 = (bf16[1,512,2048]{2,1,0:T(8,128)(2,1)S(1)}, bf16[1,512,2048]{2,1,0:T(8,128)(2,1)}, u32[]{:S(2)}) copy-start(bf16[1,512,2048]{2,1,0:T(8,128)(2,1)} %param.12) | copy-start | bytes 6291460
Sparse Core Ops, SparseCore 0:
  16.8 81.7 all-gather.7
  101.1 50.6 all-gather.5
  155.7 86.9 reduce-scatter.1
  244.9 67.9 all-reduce.1
  315.3 81.3 all-gather.9
where the time goes:
time: 470 us; the launch traced here: 466 us
  waiting for transfers between devices  297 us (63%)
  other arithmetic  78 us (17%)
  matrix products  44.3 us (9%)
  local copies, waits for them, and re-layouts  31.5 us (7%)
  between operations  14 us (3%)
    all_gather x2, waiting for transfers between devices, prefix(): pieces = lax.all_gather(value, axis)  156 us
    reduce_scatter x1, waiting for transfers between devices, on_device(): lax.psum_scatter((lax.dot_general(attended, grad_flat, (((0,), (0,)), (()...  83.8 us
    select_n x62, other arithmetic, turn(): return jnp.where(position < mine, longer, so_far)  76.3 us
    psum x1, waiting for transfers between devices, on_device(): weight_grad = lax.psum(group_part, 'dp').astype(jnp.float32)  53.3 us
    unnamed x26, local copies, waits for them, and re-layouts  14.9 us
    rev x1, local copies, waits for them, and re-layouts, prefix(): pieces = pieces[::-1]  11.6 us
  transfers between devices with their start and end apart: 5, of which 5 were waited for; matrix products, arithmetic and copies ran while one was open for 17% of the time, Pallas kernels for 0%

commit v1 on v0

--- a/solution.py
+++ b/solution.py
@@ -102,7 +102,12 @@
         scatter_dimension=0,
         tiled=True,
     )
-    weight_grad = lax.psum(group_part, "dp").astype(jnp.float32)
+
+    def compute_members_all_here(xin, axis_name):
+        taken_in = jax.lax.all_gather(xin, axis_name=axis_name)
+        return jnp.sum(taken_in, axis=0)
+
+    weight_grad = compute_members_all_here(group_part, "dp").astype(jnp.float32)
     return (output[None], query_grad[None], key_grad[None], value_grad[None], weight_grad)
 
 

time: 470 us -> 400 us (0.85)
  waiting for transfers between devices: 297 us -> 226 us
    psum x1 -> x0, waiting for transfers between devices: 53.3 us -> none  [on_device(): weight_grad = lax.psum(group_part, 'dp').astype(jnp.float32)]
    reduce_scatter x1, waiting for transfers between devices: 83.8 us -> 66.8 us  [on_device(): lax.psum_scatter((lax.dot_general(attended, grad_flat, (((0,), (0,)), (()...]
  transfers between devices with their start and end apart: 5 -> 5, of which waited for: 5 -> 4; matrix products, arithmetic and copies ran while one was open for 17% -> 36% of each run, Pallas kernels for 0% -> 0%
where the time goes in v1:
time: 400 us; the launch traced here: 396 us
  waiting for transfers between devices  226 us (56%)
  other arithmetic  78.5 us (20%)
  matrix products  44.5 us (11%)
  local copies, waits for them, and re-layouts  31.5 us (8%)
  between operations  14 us (4%)
    all_gather x2, waiting for transfers between devices, prefix(): pieces = lax.all_gather(value, axis)  155 us
    select_n x62, other arithmetic, turn(): return jnp.where(position < mine, longer, so_far)  76.3 us
    reduce_scatter x1, waiting for transfers between devices, on_device(): lax.psum_scatter((lax.dot_general(attended, grad_flat, (((0,), (0,)), (()...  66.8 us
    unnamed x26, local copies, waits for them, and re-layouts  14.8 us
    rev x1, local copies, waits for them, and re-layouts, prefix(): pieces = pieces[::-1]  11.6 us
  transfers between devices with their start and end apart: 5, of which 4 were waited for; matrix products, arithmetic and copies ran while one was open for 36% of the time, Pallas kernels for 0%

profile of v1, /device:TPU:1, one launch (start us, length us, event | category | flops | bytes accessed | tf_op | source)
XLA Modules:
  0.0 396.2 jit_solution(10047399886816438667)
XLA Ops:
  7.2 1.6 copy.59
  8.9 2.9 copy.58
  11.7 2.4 copy.35
  14.1 2.5 fusion.16
  17.6 2.5 copy.57
  20.0 5.0 %select_convert_fusion.1 = bf16[8,512,512]{2,1,0:T(8,128)(2,1)} fusion(pred[512,512]{1,0:T(8,128)(4,1)S(1)} %iota_compare_fusion, bf16[512,8,128]{2,1,0:T(8,128)(2,1)} %bitcast.84, bf16[512,8,128]{2,1,0:T(8,128)(2,1)} %bitcast.79), kind=kOutput, calls=%fused_computation.4 | convolution fusion | flops 543162368 | bytes 6553600 | tf_op jit(solution)/shard_map/thd,shd->hts/dot_general | solution.py:60
  25.0 73.5 %all-gather.10.cloned.1.call-done = f32[256,128,128]{2,1,0:T(8,128)} async-done(((f32[8,128,128]{2,1,0:T(8,128)}), f32[256,128,128]{2,1,0:T(8,128)}) %all-gather.10.cloned.1.call-update) | async-done | bytes 16777232 | tf_op jit(solution)/shard_map/all_gather | solution.py:13
  98.5 38.9 %while.28 = (s32[]{:T(128)}, f32[8,128,128]{2,1,0:T(8,128)S(1)}, s32[]{:T(128)}, f32[32,8,128,128]{3,2,1,0:T(8,128)}, s32[]{:T(128)}, /*index=5*/s32[]{:T(128)}) while((s32[]{:T(128)}, f32[8,128,128]{2,1,0:T(8,128)S(1)}, s32[]{:T(128)}, f32[32,8,128,128]{3,2,1,0:T(8,128)}, s32[]{:T(128)}, /*index=5*/s32[]{:T(128)}) %tuple.81), condition=%wide.region_1.2_spmd.clone, body=%wide.region_0.1_spmd.clone.sunk | while | flops 393220 | bytes 1572957 | solution.py:23
  99.8 1.2 add_select_fusion.4
  101.0 1.2 add_select_fusion.4
  102.3 1.2 add_select_fusion.4
  103.5 1.2 add_select_fusion.4
  104.8 1.2 add_select_fusion.4
  106.0 1.2 add_select_fusion.4
  107.3 1.2 add_select_fusion.4
  108.5 1.2 add_select_fusion.4
  109.8 1.2 add_select_fusion.4
  111.0 1.2 add_select_fusion.4
  112.3 1.2 add_select_fusion.4
  113.5 1.2 add_select_fusion.4
  114.8 1.2 add_select_fusion.4
  116.0 1.2 add_select_fusion.4
  117.3 1.2 add_select_fusion.4
  118.6 1.2 add_select_fusion.4
  119.8 1.2 add_select_fusion.4
  121.1 1.2 add_select_fusion.4
  122.3 1.2 add_select_fusion.4
  123.6 1.2 add_select_fusion.4
  124.8 1.2 add_select_fusion.4
  126.1 1.2 add_select_fusion.4
  127.3 1.2 add_select_fusion.4
  134.9 1.3 add_select_fusion.4
  136.2 1.2 add_select_fusion.4
  137.5 1.8 fusion.21
  139.3 3.8 fusion.6
  144.2 4.3 %multiply_convert_fusion = bf16[1024,2048]{1,0:T(8,128)(2,1)} fusion(bf16[512,1024]{0,1:T(8,128)(2,1)S(1)} %bitcast.93, bf16[1,512,2048]{2,1,0:T(8,128)(2,1)S(1)} %copy-done), kind=kOutput, calls=%fused_computation.2 | convolution fusion | flops 2151677952 | bytes 7340032 | tf_op jit(solution)/shard_map/dot_general | solution.py:96
  148.6 3.2 all-gather.8.cloned.1.call-done
  151.7 5.5 %fusion.7 = bf16[512,1024]{1,0:T(8,128)(2,1)} fusion(bf16[1024,2048]{1,0:T(8,128)(2,1)} %all-gather.8.cloned.1.call-done, bf16[1,512,2048]{2,1,0:T(8,128)(2,1)S(1)} %copy-done), kind=kOutput, calls=%fused_computation.17 | convolution fusion | flops 2148007936 | bytes 7340032 | tf_op jit(solution)/shard_map/dot_general | solution.py:43
  157.3 1.6 copy.56
  158.9 1.7 convolution_bitcast_fusion
  161.8 1.6 select_convert_fusion
  164.0 2.0 fusion.28
  166.7 1.5 fusion.2
  168.2 1.3 copy.51
  169.5 6.3 %fusion = bf16[1,512,2048]{2,1,0:T(8,128)(2,1)} fusion(bf16[512,1024]{0,1:T(8,128)(2,1)} %bitcast.94, bf16[1024,2048]{1,0:T(8,128)(2,1)} %all-gather.8.cloned.1.call-done), kind=kOutput, calls=%fused_computation.6 | convolution fusion | flops 2148532224 | bytes 7340032 | tf_op jit(solution)/shard_map/dot_general | solution.py:70
  175.9 66.8 %reduce-scatter.2.cloned.1.call-done = bf16[32,2048]{1,0:T(8,128)(2,1)} async-done(((bf16[1024,2048]{1,0:T(8,128)(2,1)}), bf16[32,2048]{1,0:T(8,128)(2,1)}) %reduce-scatter.2.cloned.1.call-update) | async-done | bytes 131088 | tf_op jit(solution)/shard_map/reduce_scatter | solution.py:94
  242.7 81.7 %all-gather.12.cloned.1.call-done = f32[256,128,128]{2,1,0:T(8,128)} async-done(((f32[8,128,128]{2,1,0:T(8,128)}), f32[256,128,128]{2,1,0:T(8,128)}) %all-gather.12.cloned.1.call-update) | async-done | bytes 16777232 | tf_op jit(solution)/shard_map/all_gather | solution.py:13
  324.4 11.6 %rev.3 = f32[32,8,128,128]{3,2,1,0:T(8,128)} reverse(f32[32,8,128,128]{3,2,1,0:T(8,128)} %bitcast.74), dimensions={0} | reverse | bytes 33554432 | tf_op jit(solution)/shard_map/rev | solution.py:15
  336.0 38.9 %while.29 = (s32[]{:T(128)}, f32[8,128,128]{2,1,0:T(8,128)S(1)}, s32[]{:T(128)}, f32[32,8,128,128]{3,2,1,0:T(8,128)}, s32[]{:T(128)}, /*index=5*/s32[]{:T(128)}) while((s32[]{:T(128)}, f32[8,128,128]{2,1,0:T(8,128)S(1)}, s32[]{:T(128)}, f32[32,8,128,128]{3,2,1,0:T(8,128)}, s32[]{:T(128)}, /*index=5*/s32[]{:T(128)}) %tuple.68), condition=%wide.region_3.4_spmd.clone, body=%wide.region_2.3_spmd.clone.sunk | while | flops 393220 | bytes 1572957 | solution.py:23
  336.0 1.3 add_select_fusion.5
  343.6 1.2 add_select_fusion.5
  344.9 1.2 add_select_fusion.5
  346.1 1.2 add_select_fusion.5
  347.4 1.2 add_select_fusion.5
  349.9 1.2 add_select_fusion.5
  352.4 1.2 add_select_fusion.5
  354.9 1.2 add_select_fusion.5
  356.2 1.2 add_select_fusion.5
  368.7 1.2 add_select_fusion.5
  375.4 4.1 %fusion.1 = bf16[512,8,128]{0,2,1:T(8,128)(2,1)} fusion(f32[8,128,512]{2,1,0:T(8,128)S(1)} %fusion.13, bf16[8,512,512]{2,1,0:T(8,128)(2,1)} %copy-done.3, bf16[512,8,128]{2,1,0:T(8,128)(2,1)S(1)} %bitcast.82), kind=kOutput, calls=%fused_computation.8 | convolution fusion | flops 538443776 | bytes 8388608 | tf_op jit(solution)/shard_map/hts,thd->shd/dot_general | solution.py:81
  379.5 2.4 copy.52
  381.9 3.5 add_convert_fusion
  385.3 2.3 copy.53
  387.6 1.4 reduce_sum.12
  (65 shorter events, 38.8 us)
Async XLA Ops:
  7.2 137.0 %copy-start = (bf16[1,512,2048]{2,1,0:T(8,128)(2,1)S(1)}, bf16[1,512,2048]{2,1,0:T(8,128)(2,1)}, u32[]{:S(2)}) copy-start(bf16[1,512,2048]{2,1,0:T(8,128)(2,1)} %param.12) | copy-start | bytes 6291460
  7.2 91.3 %all-gather.10.cloned.1.call-start = ((), (), s32[]{:S(2)}) async-start(), calls=%async_computation.3 | async-start | bytes 17301504 | tf_op jit(solution)/shard_map/all_gather | solution.py:13
  8.9 8.6 %copy-start.4 = (bf16[64,8,8,128]{3,2,1,0:T(8,128)(2,1)}, bf16[64,8,8,128]{3,2,1,0:T(8,128)(2,1)S(1)}, u32[]{:S(2)}) copy-start(bf16[64,8,8,128]{3,2,1,0:T(8,128)(2,1)S(1)} %copy.59) | copy-start | bytes 3145732
  16.6 135.1 %all-gather.8.cloned.1.call-start = ((), (), s32[]{:S(2)}) async-start(), calls=%async_computation.1 | async-start | bytes 4325376 | tf_op jit(solution)/shard_map/all_gather | solution.py:42
  17.4 225.3 %reduce-scatter.2.cloned.1.call-start = ((), (), s32[]{:S(2)}) async-start(), calls=%async_computation.2 | async-start | bytes 4325376 | tf_op jit(solution)/shard_map/reduce_scatter | solution.py:94
  137.5 1.8 copy-start.5
  143.1 1.0 copy-start.9
  148.5 175.8 %all-gather.12.cloned.1.call-start = ((), (), s32[]{:S(2)}) async-start(), calls=%async_computation.4 | async-start | bytes 17301504 | tf_op jit(solution)/shard_map/all_gather | solution.py:13
  157.3 4.5 %copy-start.6 = (bf16[64,8,8,128]{3,2,1,0:T(8,128)(2,1)S(1)}, bf16[64,8,8,128]{3,2,1,0:T(8,128)(2,1)}, u32[]{:S(2)}) copy-start(bf16[64,8,8,128]{3,2,1,0:T(8,128)(2,1)} %copy-done.4) | copy-start | bytes 3145732
  161.6 226.0 %all-gather.14.cloned.1.call-start = ((), (), s32[]{:S(2)}) async-start(), calls=%async_computation.5 | async-start | bytes 1179648 | tf_op jit(solution)/shard_map/all_gather | solution.py:107
  161.8 2.2 copy-start.2
  164.0 2.7 copy-start.3
  164.0 2.7 copy-start.8
  336.0 39.4 %copy-start.7 = (bf16[64,8,8,128]{3,2,1,0:T(8,128)(2,1)S(1)}, bf16[64,8,8,128]{3,2,1,0:T(8,128)(2,1)}, u32[]{:S(2)}) copy-start(bf16[64,8,8,128]{3,2,1,0:T(8,128)(2,1)} %copy.57) | copy-start | bytes 3145732
  379.5 10.2 %copy-start.1 = (bf16[1,512,2048]{2,1,0:T(8,128)(2,1)S(1)}, bf16[1,512,2048]{2,1,0:T(8,128)(2,1)}, u32[]{:S(2)}) copy-start(bf16[1,512,2048]{2,1,0:T(8,128)(2,1)} %param.12) | copy-start | bytes 6291460
Sparse Core Ops, SparseCore 0:
  16.8 81.7 all-gather.9
  101.1 50.6 all-gather.7
  155.7 86.9 reduce-scatter.1
  245.4 78.9 all-gather.11
  326.1 32.7 all-gather.13
